TPU v7x, 128 devices: a whole 4x4x4 slice. The times are simulated.
128 devices in a mesh: grp: 2 (over y_lo), row: 16 (over x, z), hid: 4 (over y_hi, core).
Axes of the slice: x: 4, y: 4 (y_hi: 2, y_lo: 2; y = y_hi * 2 + y_lo), z: 4, core: 2. Of those that a mesh axis runs over, the one named last changes fastest.
Arguments:
- token_ids: int32 [512, 64], P(('grp', 'row')), may hold values from 0 to 128255, as said below
- activations: bfloat16 [512, 64, 4096], P(('grp', 'row'), None, 'hid'), may hold values from -6 to 6
- out_grads: bfloat16 [512, 64, 4096], P(('grp', 'row'), None, 'hid'), may hold values from -6 to 6
- proj_in: bfloat16 [64, 4096], P(None, 'hid'), may hold values from -0.09375 to 0.09375
- proj_out: bfloat16 [64, 4096], P(None, 'hid'), may hold values from -0.09375 to 0.09375
- inverse_curvature: float32 [4096, 4096], P('row', ('grp', 'hid')), as said below
- store_grads: bfloat16 [262144, 4096], P(('grp', 'row', 'hid')), may hold values from -1 to 1
- store_order: int32 [262144], P(('grp', 'row', 'hid')), may hold values from 0 to 262143, each once
- example_ids: int32 [512], replicated, may hold values from 0 to 262143
Outputs:
- scores: bfloat16 [262144, 512], P(('grp', 'row', 'hid'))
Inputs may be any that keep to these rules, and one draw needn't show every extreme that they name: `token_ids`: 0 marks padding, which only follows a query's tokens; each query has at least 16 tokens that are not padding. `example_ids`: each query's id names a stored example. `inverse_curvature`: symmetric.
All inputs are finite; a program needn't handle non-finite values.
Results may differ from a plain program's by a relative error of at most 0.013.
Values may be sent and summed in bfloat16 or wider, within the bound.
No kernel may reach another device: no remote copies, remote signals or barrier semaphores. Data moves between devices by JAX's collectives and lax.ppermute only.
A program may use at most 128 MiB of HBM per device.

v0:
```python
import jax
import jax.numpy as jnp
from jax import lax
from jax.sharding import PartitionSpec as P


def copy_for_each(value, axis):
    devices = lax.axis_size(axis)
    return lax.all_to_all(
        jnp.broadcast_to(value[None], (devices, *value.shape)), axis, 0, 0, tiled=True
    )


def over_copies(value, axis):
    everything = copy_for_each(value, axis)
    return jnp.sum(everything, axis=0)


def laid_out(blocks, dim):
    blocks = jnp.moveaxis(blocks, 0, dim)
    lengths = blocks.shape
    return blocks.reshape(*lengths[:dim], lengths[dim] * lengths[dim + 1], *lengths[dim + 2 :])


def collect(value, axis, dim):
    return laid_out(copy_for_each(value, axis), dim)


def in_blocks(value, dim, devices):
    before, after = (value.shape[:dim], value.shape[dim + 1 :])
    return jnp.moveaxis(value.reshape(*before, devices, -1, *after), dim, 0)


def sent_and_summed(value, axis, dim):
    blocks = in_blocks(value, dim, lax.axis_size(axis))
    arrived = lax.all_to_all(blocks, axis, split_axis=0, concat_axis=0, tiled=True)
    return arrived.sum(axis=0)


def local(
    token_ids,
    activations,
    out_grads,
    proj_in,
    proj_out,
    inverse_curvature,
    store_grads,
    store_order,
    example_ids,
):
    queries_here, query_tokens, width_here = activations.shape
    rank_side = proj_in.shape[0]
    contract = (((1,), (1,)), ((), ()))
    flat_inputs = activations.reshape(queries_here * query_tokens, width_here)
    flat_grads = out_grads.reshape(queries_here * query_tokens, width_here)
    out_part = lax.dot_general(flat_grads, proj_out, contract, preferred_element_type=jnp.float32)
    in_part = lax.dot_general(flat_inputs, proj_in, contract, preferred_element_type=jnp.float32)
    projected = jnp.concatenate([out_part, in_part], axis=1)
    projected = over_copies(projected, "hid")
    out_side = projected[:, :rank_side].reshape(queries_here, query_tokens, rank_side)
    in_side = projected[:, rank_side:].reshape(queries_here, query_tokens, rank_side)
    usable = (token_ids > 0).astype(jnp.float32)
    counted = jnp.sum(usable, axis=1, keepdims=True)
    weights = usable / counted
    scaled = out_side * weights[:, :, None]
    query_grads = jnp.einsum("qla,qlb->qab", scaled, in_side).reshape(
        queries_here, rank_side * rank_side
    )
    query_block = lax.all_to_all(query_grads, "row", split_axis=1, concat_axis=0, tiled=True)
    query_block = collect(query_block, "grp", 0)
    partial_value = jnp.dot(
        query_block,
        inverse_curvature,
        precision=lax.Precision.HIGHEST,
        preferred_element_type=jnp.float32,
    )
    pre_share = sent_and_summed(partial_value, "row", 0).astype(jnp.bfloat16)
    pre_share = collect(pre_share, ("grp", "hid"), 1)
    scores = lax.dot_general(
        store_grads,
        lax.all_gather(pre_share, "row", axis=0, tiled=True),
        contract,
        preferred_element_type=jnp.float32,
    )
    is_self = store_order[:, None] == example_ids[None, :]
    return jnp.where(is_self, 0.0, scores).astype(jnp.bfloat16)


def solution(mesh):
    placed = (
        P(("grp", "row"), None),
        P(("grp", "row"), None, "hid"),
        P(("grp", "row"), None, "hid"),
        P(None, "hid"),
        P(None, "hid"),
        P("row", ("grp", "hid")),
        P(("grp", "row", "hid"), None),
        P(("grp", "row", "hid")),
        P(),
    )
    return jax.shard_map(
        local, mesh=mesh, in_specs=placed, out_specs=P(("grp", "row", "hid"), None), check_vma=False
    )
```

profile of v0, /device:TPU:1, one launch (start us, length us, event | category | flops | bytes accessed | tf_op | source)
XLA Modules:
  0.0 177.7 jit_solution(14987090511426984861)
XLA Ops:
  6.5 1.6 copy-done
  8.1 1.7 fusion.6
  9.8 2.4 %fusion.5 = f32[1024,64]{0,1:T(8,128)S(1)} fusion(bf16[1024,1024]{1,0:T(8,128)(2,1)} %bitcast.29, bf16[64,1024]{1,0:T(8,128)(2,1)} %param.13), kind=kOutput, calls=%fused_computation.11 | convolution fusion | flops 134217728 | bytes 2490368 | tf_op jit(solution)/shard_map/dot_general | solution.py:56
  12.2 0.2 copy.23
  12.4 1.5 broadcast_in_dim.12
  13.9 6.0 %all-to-all-start = ((f32[4,1024,128]{2,1,0:T(8,128)}), f32[4,1024,128]{2,1,0:T(8,128)}, u32[]{:S(2)}, u32[]{:S(2)}) async-start(f32[4,1024,128]{2,1,0:T(8,128)} %broadcast_in_dim.12), calls=%async_computation | async-start | bytes 4194304 | tf_op jit(solution)/shard_map/all_to_all | solution.py:9
  19.8 0.1 convert_reduce_fusion
  19.9 0.1 convert_divide_fusion
  20.0 26.1 %all-to-all-done = f32[4,1024,128]{2,1,0:T(8,128)} async-done(((f32[4,1024,128]{2,1,0:T(8,128)}), f32[4,1024,128]{2,1,0:T(8,128)}, u32[]{:S(2)}, u32[]{:S(2)}) %all-to-all-start) | async-done | bytes 2097184 | tf_op jit(solution)/shard_map/all_to_all | solution.py:9
  46.1 1.8 reduce_sum.27
  47.9 0.1 slice.9
  48.0 0.3 copy.29
  48.4 0.2 fusion.3
  48.6 0.2 all_to_all.25
  48.8 0.2 copy.26
  48.9 14.9 %all_to_all.36 = f32[16,16,256]{2,0,1:T(8,128)S(1)} all-to-all(f32[16,16,256]{2,0,1:T(8,128)S(1)} %copy.26), channel_id=1, replica_groups=mesh['grp'=2,'row'=16,'hid'=4] {'row'}, dimensions={1} | all-to-all | bytes 524288 | tf_op jit(solution)/shard_map/all_to_all | solution.py:69
  63.8 7.8 %all_to_all.37 = f32[2,256,256]{2,1,0:T(8,128)S(1)} all-to-all(f32[2,256,256]{2,1,0:T(8,128)S(1)} %broadcast_in_dim.14), channel_id=1, replica_groups=mesh['grp'=2,'row'=16,'hid'=4] {'grp'}, dimensions={0} | all-to-all | bytes 1048576 | tf_op jit(solution)/shard_map/all_to_all | solution.py:9
  71.7 1.0 fusion.1
  72.7 17.1 %all_to_all.38 = f32[16,32,512]{2,1,0:T(8,128)S(1)} all-to-all(f32[16,32,512]{2,1,0:T(8,128)S(1)} %fusion.1), channel_id=1, replica_groups=mesh['grp'=2,'row'=16,'hid'=4] {'row'}, dimensions={0} | all-to-all | bytes 2097152 | tf_op jit(solution)/shard_map/all_to_all | solution.py:36
  89.9 13.6 %all_to_all.39 = bf16[8,32,512]{2,1,0:T(8,128)(2,1)S(1)} all-to-all(bf16[8,32,512]{2,1,0:T(8,128)(2,1)S(1)} %broadcast_in_dim.15), channel_id=1, replica_groups=mesh['grp'=2,'row'=16,'hid'=4] {'grp','hid'}, dimensions={0} | all-to-all | bytes 524288 | tf_op jit(solution)/shard_map/all_to_all | solution.py:9
  103.5 0.7 copy.30
  104.3 48.0 %all-gather.2.cloned.1.call-done = bf16[512,4096]{1,0:T(8,128)(2,1)} async-done(((bf16[32,4096]{1,0:T(8,128)(2,1)}), bf16[512,4096]{1,0:T(8,128)(2,1)}) %all-gather.2.cloned.1.call-update) | async-done | bytes 4194320 | tf_op jit(solution)/shard_map/all_gather | solution.py:81
  152.3 14.7 %fusion = bf16[2048,512]{0,1:T(8,128)(2,1)} fusion(bf16[512,4096]{1,0:T(8,128)(2,1)} %all-gather.2.cloned.1.call-done, bf16[2048,4096]{1,0:T(8,128)(2,1)} %param.15, s32[2048]{0:T(1024)S(1)} %copy-done.3, s32[512]{0:T(512)S(1)} %copy-done.4), kind=kOutput, calls=%fused_computation.1 | convolution fusion | flops 8593080320 | bytes 23078912 | tf_op jit(solution)/shard_map/dot_general | solution.py:79
  166.9 3.9 %copy.28 = bf16[2048,512]{1,0:T(8,128)(2,1)} copy(bf16[2048,512]{0,1:T(8,128)(2,1)} %fusion) | data formatting | bytes 4194304 | tf_op jit(solution)/shard_map/convert_element_type | solution.py:86
  (16 shorter events, 0.3 us)
Async XLA Ops:
  6.5 1.6 copy-start
  12.2 7.6 %copy-start.2 = (s32[16,64]{1,0:T(8,128)S(1)}, s32[16,64]{1,0:T(8,128)}, u32[]{:S(2)}) copy-start(s32[16,64]{1,0:T(8,128)} %param.9) | copy-start | bytes 12292
  13.9 32.3 %all-to-all-start = ((f32[4,1024,128]{2,1,0:T(8,128)}), f32[4,1024,128]{2,1,0:T(8,128)}, u32[]{:S(2)}, u32[]{:S(2)}) async-start(f32[4,1024,128]{2,1,0:T(8,128)} %broadcast_in_dim.12), calls=%async_computation | async-start | bytes 4194304 | tf_op jit(solution)/shard_map/all_to_all | solution.py:9
  19.8 132.4 %all-gather.2.cloned.1.call-start = ((), (), s32[]{:S(2)}) async-start(), calls=%async_computation.5 | async-start | bytes 4456448 | tf_op jit(solution)/shard_map/all_gather | solution.py:81
  48.4 23.3 %copy-start.1 = (f32[256,512]{1,0:T(8,128)S(1)}, f32[256,512]{1,0:T(8,128)}, u32[]{:S(2)}) copy-start(f32[256,512]{1,0:T(8,128)} %param.14) | copy-start | bytes 1572868
  63.8 88.4 %copy-start.3 = (s32[2048]{0:T(1024)S(1)}, s32[2048]{0:T(1024)}, u32[]{:S(2)}) copy-start(s32[2048]{0:T(1024)} %param.16) | copy-start | bytes 24580
  63.8 88.4 %copy-start.4 = (s32[512]{0:T(512)S(1)}, s32[512]{0:T(512)}, u32[]{:S(2)}) copy-start(s32[512]{0:T(512)} %param.17) | copy-start | bytes 6148
Sparse Core Ops, SparseCore 0:
  104.4 47.7 all-gather.1
where the time goes:
time: 178 us
  waiting for transfers between devices  74.1 us (42%)
  blocking collectives  53.4 us (30%)
  matrix products  19.9 us (11%)
  between operations  13.5 us (8%)
  local copies, waits for them, and re-layouts  8.71 us (5%)
  starting transfers between devices  5.96 us (3%)
  other arithmetic  2.11 us (1%)
    all_gather x1, waiting for transfers between devices, local(): lax.all_gather(pre_share, 'row', axis=0, tiled=True)  48 us
    all_to_all x1, waiting for transfers between devices, copy_for_each(): lax.all_to_all(jnp.broadcast_to(value[None], (devices, *value.shape)), ax...  26.1 us
    all_to_all x2, blocking collectives, copy_for_each(): lax.all_to_all(jnp.broadcast_to(value[None], (devices, *value.shape)), ax...  21.5 us
    all_to_all x1, blocking collectives, sent_and_summed(): lax.all_to_all(blocks, axis, split_axis=0, concat_axis=0, tiled=True)  17.1 us
    all_to_all x1, blocking collectives, local(): lax.all_to_all(query_grads, 'row', split_axis=1, concat_axis=0, tiled=True)  14.9 us
    dot_general x1, matrix products, local(): lax.dot_general(store_grads, lax.all_gather(pre_share, 'row', axis=0, til...  14.7 us
    all_to_all x1, starting transfers between devices, copy_for_each(): lax.all_to_all(jnp.broadcast_to(value[None], (devices, *value.shape)), ax...  5.95 us
    convert_element_type x1, local copies, waits for them, and re-layouts, local(): return jnp.where(is_self, 0.0, scores).astype(jnp.bfloat16)  3.92 us
  transfers between devices with their start and end apart: 2, of which 2 were waited for; matrix products, arithmetic and copies ran while one was open for 0% of the time, Pallas kernels for 0%

commit v1 on v0

--- a/solution.py
+++ b/solution.py
@@ -78,7 +78,9 @@
     pre_share = collect(pre_share, ("grp", "hid"), 1)
     scores = lax.dot_general(
         store_grads,
-        lax.all_gather(pre_share, "row", axis=0, tiled=True),
+        jnp.concatenate(
+            lax.all_to_all(jnp.stack([pre_share] * lax.axis_size("row")), "row", 0, 0), axis=0
+        ),
         contract,
         preferred_element_type=jnp.float32,
     )

time: 178 us -> 169 us (0.949)
  blocking collectives: 53.4 us -> 106 us
  waiting for transfers between devices: 74.1 us -> 26.1 us
  between operations: 13.5 us -> 0.13 us
    all_to_all x0 -> x1, blocking collectives: none -> 52.7 us  [local(): lax.all_to_all(jnp.stack([pre_share] * lax.axis_size('row')), 'row', 0, 0)]
    all_gather x1 -> x0, waiting for transfers between devices: 48 us -> none  [local(): lax.all_gather(pre_share, 'row', axis=0, tiled=True)]
  transfers between devices with their start and end apart: 2 -> 1, of which waited for: 2 -> 1; matrix products, arithmetic and copies ran while one was open for 0% -> 0% of each run, Pallas kernels for 0% -> 0%
where the time goes in v1:
time: 169 us; the launch traced here: 168 us
  blocking collectives  106 us (63%)
  waiting for transfers between devices  26.1 us (15%)
  matrix products  18.7 us (11%)
  local copies, waits for them, and re-layouts  8.5 us (5%)
  starting transfers between devices  5.95 us (4%)
  other arithmetic  2.11 us (1%)
    all_to_all x1, blocking collectives, local(): lax.all_to_all(jnp.stack([pre_share] * lax.axis_size('row')), 'row', 0, 0)  52.7 us
    all_to_all x1, waiting for transfers between devices, copy_for_each(): lax.all_to_all(jnp.broadcast_to(value[None], (devices, *value.shape)), ax...  26.1 us
    all_to_all x2, blocking collectives, copy_for_each(): lax.all_to_all(jnp.broadcast_to(value[None], (devices, *value.shape)), ax...  21.5 us
    all_to_all x1, blocking collectives, sent_and_summed(): lax.all_to_all(blocks, axis, split_axis=0, concat_axis=0, tiled=True)  17.1 us
    all_to_all x1, blocking collectives, local(): lax.all_to_all(query_grads, 'row', split_axis=1, concat_axis=0, tiled=True)  14.9 us
    dot_general x1, matrix products, local(): lax.dot_general(store_grads, jnp.concatenate(lax.all_to_all(jnp.stack([pr...  13.5 us
    all_to_all x1, starting transfers between devices, copy_for_each(): lax.all_to_all(jnp.broadcast_to(value[None], (devices, *value.shape)), ax...  5.95 us
    convert_element_type x1, local copies, waits for them, and re-layouts, local(): return jnp.where(is_self, 0.0, scores).astype(jnp.bfloat16)  3.92 us
  transfers between devices with their start and end apart: 1, of which 1 were waited for; matrix products, arithmetic and copies ran while one was open for 0% of the time, Pallas kernels for 0%

profile of v1, /device:TPU:1, one launch (start us, length us, event | category | flops | bytes accessed | tf_op | source)
XLA Modules:
  0.0 167.6 jit_solution(13074667267413160068)
XLA Ops:
  0.0 1.6 copy-done
  1.6 1.7 fusion.6
  3.3 2.4 %fusion.5 = f32[1024,64]{0,1:T(8,128)S(1)} fusion(bf16[1024,1024]{1,0:T(8,128)(2,1)} %bitcast.31, bf16[64,1024]{1,0:T(8,128)(2,1)} %param.13), kind=kOutput, calls=%fused_computation.11 | convolution fusion | flops 134217728 | bytes 2490368 | tf_op jit(solution)/shard_map/dot_general | solution.py:56
  5.7 0.2 copy.23
  5.9 1.5 broadcast_in_dim.12
  7.3 6.0 %all-to-all-start = ((f32[4,1024,128]{2,1,0:T(8,128)}), f32[4,1024,128]{2,1,0:T(8,128)}, u32[]{:S(2)}, u32[]{:S(2)}) async-start(f32[4,1024,128]{2,1,0:T(8,128)} %broadcast_in_dim.12), calls=%async_computation | async-start | bytes 4194304 | tf_op jit(solution)/shard_map/all_to_all | solution.py:9
  13.3 0.1 convert_reduce_fusion
  13.4 0.1 convert_divide_fusion
  13.5 26.1 %all-to-all-done = f32[4,1024,128]{2,1,0:T(8,128)} async-done(((f32[4,1024,128]{2,1,0:T(8,128)}), f32[4,1024,128]{2,1,0:T(8,128)}, u32[]{:S(2)}, u32[]{:S(2)}) %all-to-all-start) | async-done | bytes 2097184 | tf_op jit(solution)/shard_map/all_to_all | solution.py:9
  39.6 1.8 %reduce_sum.27 = f32[1024,128]{1,0:T(8,128)S(1)} reduce(f32[4,1024,128]{2,1,0:T(8,128)} %all-to-all-done, f32[]{:T(128)} %constant.0.clone.1), dimensions={0}, to_apply=%region_0.0 | reduce | flops 393216 | bytes 2621444 | tf_op jit(solution)/shard_map/reduce_sum | solution.py:16
  41.4 0.1 slice.9
  41.5 0.3 copy.29
  41.8 0.2 fusion.3
  42.1 0.2 all_to_all.28
  42.2 0.2 copy.26
  42.4 14.9 %all_to_all.41 = f32[16,16,256]{2,0,1:T(8,128)S(1)} all-to-all(f32[16,16,256]{2,0,1:T(8,128)S(1)} %copy.26), channel_id=1, replica_groups=mesh['grp'=2,'row'=16,'hid'=4] {'row'}, dimensions={1} | all-to-all | bytes 524288 | tf_op jit(solution)/shard_map/all_to_all | solution.py:69
  57.3 7.8 %all_to_all.42 = f32[2,256,256]{2,1,0:T(8,128)S(1)} all-to-all(f32[2,256,256]{2,1,0:T(8,128)S(1)} %broadcast_in_dim.14), channel_id=1, replica_groups=mesh['grp'=2,'row'=16,'hid'=4] {'grp'}, dimensions={0} | all-to-all | bytes 1048576 | tf_op jit(solution)/shard_map/all_to_all | solution.py:9
  65.2 1.0 fusion.1
  66.2 17.1 %all_to_all.43 = f32[16,32,512]{2,1,0:T(8,128)S(1)} all-to-all(f32[16,32,512]{2,1,0:T(8,128)S(1)} %fusion.1), channel_id=1, replica_groups=mesh['grp'=2,'row'=16,'hid'=4] {'row'}, dimensions={0} | all-to-all | bytes 2097152 | tf_op jit(solution)/shard_map/all_to_all | solution.py:36
  83.4 13.6 %all_to_all.44 = bf16[8,32,512]{2,1,0:T(8,128)(2,1)S(1)} all-to-all(bf16[8,32,512]{2,1,0:T(8,128)(2,1)S(1)} %broadcast_in_dim.15), channel_id=1, replica_groups=mesh['grp'=2,'row'=16,'hid'=4] {'grp','hid'}, dimensions={0} | all-to-all | bytes 524288 | tf_op jit(solution)/shard_map/all_to_all | solution.py:9
  97.0 0.5 stack.3
  97.6 52.7 %all_to_all.45 = bf16[16,32,4096]{2,1,0:T(8,128)(2,1)S(1)} all-to-all(bf16[16,32,4096]{2,1,0:T(8,128)(2,1)S(1)} %stack.3), channel_id=1, replica_groups=mesh['grp'=2,'row'=16,'hid'=4] {'row'}, dimensions={0} | all-to-all | bytes 8388608 | tf_op jit(solution)/shard_map/all_to_all | solution.py:82
  150.3 13.5 %fusion = bf16[2048,512]{0,1:T(8,128)(2,1)} fusion(bf16[512,4096]{1,0:T(8,128)(2,1)S(1)} %bitcast.29, bf16[2048,4096]{1,0:T(8,128)(2,1)} %param.15, s32[2048]{0:T(1024)S(1)} %copy-done.3, s32[512]{0:T(512)S(1)} %copy-done.4), kind=kOutput, calls=%fused_computation.1 | convolution fusion | flops 8593080320 | bytes 23078912 | tf_op jit(solution)/shard_map/dot_general | solution.py:79
  163.7 3.9 %copy.28 = bf16[2048,512]{1,0:T(8,128)(2,1)} copy(bf16[2048,512]{0,1:T(8,128)(2,1)} %fusion) | data formatting | bytes 4194304 | tf_op jit(solution)/shard_map/convert_element_type | solution.py:88
  (15 shorter events, 0.3 us)
Async XLA Ops:
  0.0 1.6 copy-start
  5.7 7.6 %copy-start.2 = (s32[16,64]{1,0:T(8,128)S(1)}, s32[16,64]{1,0:T(8,128)}, u32[]{:S(2)}) copy-start(s32[16,64]{1,0:T(8,128)} %param.9) | copy-start | bytes 12292
  7.3 32.3 %all-to-all-start = ((f32[4,1024,128]{2,1,0:T(8,128)}), f32[4,1024,128]{2,1,0:T(8,128)}, u32[]{:S(2)}, u32[]{:S(2)}) async-start(f32[4,1024,128]{2,1,0:T(8,128)} %broadcast_in_dim.12), calls=%async_computation | async-start | bytes 4194304 | tf_op jit(solution)/shard_map/all_to_all | solution.py:9
  41.8 23.3 %copy-start.1 = (f32[256,512]{1,0:T(8,128)S(1)}, f32[256,512]{1,0:T(8,128)}, u32[]{:S(2)}) copy-start(f32[256,512]{1,0:T(8,128)} %param.14) | copy-start | bytes 1572868
  97.5 52.7 %copy-start.3 = (s32[2048]{0:T(1024)S(1)}, s32[2048]{0:T(1024)}, u32[]{:S(2)}) copy-start(s32[2048]{0:T(1024)} %param.16) | copy-start | bytes 24580
  97.5 52.7 %copy-start.4 = (s32[512]{0:T(512)S(1)}, s32[512]{0:T(512)}, u32[]{:S(2)}) copy-start(s32[512]{0:T(512)} %param.17) | copy-start | bytes 6148
